TPU v7x, 32 devices: a whole 2x2x4 slice. The times are simulated.
32 devices in a mesh: dp: 2 (over x), ctx: 4 (over y, core), tp: 4 (over z).
Axes of the slice: x: 2, y: 2, z: 4, core: 2. Of those that a mesh axis runs over, the one named last changes fastest.
Arguments:
- tokens: bfloat16 [16384, 768], P(('dp', 'ctx', 'tp')), may hold values from -6 to 6
- first_gain: bfloat16 [768], replicated, may hold values from 0.5 to 1.5
- first_bias: bfloat16 [768], replicated, may hold values from -0.4375 to 0.4375
- mixer_weight: bfloat16 [768, 3, 768], P(None, None, 'tp'), may hold values from -0.21875 to 0.21875
- mixer_bias: bfloat16 [3, 768], P(None, 'tp'), may hold values from -0.3125 to 0.3125
- feature_weight: bfloat16 [2, 12, 64, 64], P(None, 'tp'), may hold values from -1.5 to 1.5
- feature_bias: bfloat16 [2, 12, 64], P(None, 'tp'), may hold values from -6 to 6
- output_weight: bfloat16 [768, 768], P('tp'), may hold values from -6 to 6
- output_bias: bfloat16 [768], replicated, may hold values from -4 to 4
- second_gain: bfloat16 [768], replicated, may hold values from 0.5 to 1.5
- second_bias: bfloat16 [768], replicated, may hold values from -4 to 4
- inner_weight: bfloat16 [768, 3072], P(None, 'tp'), may hold values from -0.21875 to 0.21875
- inner_bias: bfloat16 [3072], P('tp'), may hold values from -4 to 4
- outer_weight: bfloat16 [3072, 768], P('tp'), may hold values from -0.109375 to 0.109375
- outer_bias: bfloat16 [768], replicated, may hold values from -4 to 4
- block_owner: int32 [2, 32], P('dp'), may hold values from 0 to 0, as said below
- cotangent: bfloat16 [16384, 768], P(('dp', 'ctx', 'tp')), may hold values from -6 to 6
Outputs:
- result: bfloat16 [16384, 768], P(('dp', 'ctx', 'tp'))
- tokens_gradient: float32 [16384, 768], P(('dp', 'ctx', 'tp'))
- first_gain_gradient: float32 [768], replicated
- first_bias_gradient: float32 [768], replicated
- mixer_weight_gradient: float32 [768, 3, 768], P(None, None, 'tp')
- mixer_bias_gradient: float32 [3, 768], P(None, 'tp')
- feature_weight_gradient: float32 [2, 12, 64, 64], P(None, 'tp')
- feature_bias_gradient: float32 [2, 12, 64], P(None, 'tp')
- output_weight_gradient: float32 [768, 768], P('tp')
- output_bias_gradient: float32 [768], replicated
- second_gain_gradient: float32 [768], replicated
- second_bias_gradient: float32 [768], replicated
- inner_weight_gradient: float32 [768, 3072], P(None, 'tp')
- inner_bias_gradient: float32 [3072], P('tp')
- outer_weight_gradient: float32 [3072, 768], P('tp')
- outer_bias_gradient: float32 [768], replicated
Inputs may be any that keep to these rules, and one draw needn't show every extreme that they name: `block_owner`: all blocks of one sequence carry one number, and pieces of a data group share the same blocks. A sequence covers 8192 // 256 or twice that many consecutive blocks of every piece, so it has 8192 or 16384 tokens; its number is the index of its last 8192-token unit, so numbers rise along a row, differ between sequences, and the last block of every row carries 1 - 1.
All inputs are finite; a program needn't handle non-finite values.
Results may differ from a plain program's by a relative error of at most 0.015.
Values may be sent and summed in bfloat16 or wider, within the bound.
A program may use at most 128 MiB of HBM per device.

v0:
```python
import jax
import jax.numpy as jnp
from jax import lax
from jax.sharding import PartitionSpec as P

HD = 64
BLOCK = 64
SHORT = 8192
EPSILON = 1e-05
HIGHEST = lax.Precision.HIGHEST


def entering(x, axis, combine, identity, reverse):
    peers, mine = (lax.axis_size(axis), lax.axis_index(axis))
    everything = jax.tree.map(lambda part: lax.all_gather(part, axis), x)
    start = jax.tree.map(
        lambda part, zero: jnp.broadcast_to(jnp.asarray(zero, part.dtype), part.shape), x, identity
    )

    def turn(k, before):
        at = peers - 1 - k if reverse else k
        reached = at > mine if reverse else at < mine
        new = combine(before, jax.tree.map(lambda part: part[at], everything))
        return jax.tree.map(lambda a, b: jnp.where(reached, a, b), new, before)

    return lax.fori_loop(0, peers, turn, start)


def layer_norm(values, norm_gain, norm_offset):
    average = jnp.mean(values, axis=-1, keepdims=True)
    centered = values - average
    variance = jnp.mean(centered * centered, axis=-1, keepdims=True)
    return centered * lax.rsqrt(variance + EPSILON) * norm_gain + norm_offset


def gaussian_unit(values):
    return (
        0.5
        * values
        * (1.0 + jnp.tanh(0.7978845608028654 * (values + 0.044715 * values * values * values)))
    )


def feature_map(inputs, weight, offset):
    logits = jnp.einsum("thd,hde->the", inputs, weight, precision=HIGHEST) + offset
    return jnp.concatenate(
        [jax.nn.softmax(logits, axis=-1), jax.nn.softmax(-logits, axis=-1)], axis=-1
    )


def rounded(values):
    return lax.optimization_barrier(values.astype(jnp.bfloat16)).astype(jnp.float32)


def add_pair(first_pair, second_pair):
    return (first_pair[0] + second_pair[0], first_pair[1] + second_pair[1])


def shards(
    tokens,
    first_gain,
    first_bias,
    mixer_weight,
    mixer_bias,
    feature_weight,
    feature_bias,
    output_weight,
    output_bias,
    second_gain,
    second_bias,
    inner_weight,
    inner_bias,
    outer_weight,
    outer_bias,
    block_owner,
    cotangent,
):
    local_rows, model_width = tokens.shape
    heads_here = mixer_weight.shape[2] // HD
    piece_rows = local_rows * lax.axis_size("tp")
    blocks = piece_rows // BLOCK
    unit_count = piece_rows * lax.axis_size("ctx") // SHORT
    owners = block_owner[0]
    block_index = jnp.arange(blocks)
    member = (owners[:, None] == jnp.arange(unit_count)[None, :]).astype(jnp.float32)
    earlier = (
        (owners[:, None] == owners[None, :]) & (block_index[:, None] > block_index[None, :])
    ).astype(jnp.float32)
    causal = jnp.arange(BLOCK)[:, None] >= jnp.arange(BLOCK)[None, :]
    inputs = tokens.astype(jnp.float32)
    first_normed, first_pull = jax.vjp(
        layer_norm, inputs, first_gain.astype(jnp.float32), first_bias.astype(jnp.float32)
    )
    first_low = first_normed.astype(jnp.bfloat16)
    first_rows = lax.all_gather(first_low, "tp", axis=0, tiled=True)
    mixer_flat = mixer_weight.reshape(model_width, -1)
    mixed_rows = jnp.dot(
        first_rows, mixer_flat, preferred_element_type=jnp.float32
    ) + mixer_bias.astype(jnp.float32).reshape(-1)
    mixed_low = mixed_rows.astype(jnp.bfloat16).reshape(piece_rows, 3, heads_here, HD)
    query_rows = mixed_low[:, 0]
    key_rows = mixed_low[:, 1]
    value_rows = mixed_low[:, 2]
    weight_float = feature_weight.astype(jnp.float32)
    bias_float = feature_bias.astype(jnp.float32)
    query_lifted, query_pull = jax.vjp(
        feature_map, query_rows.astype(jnp.float32), weight_float[0], bias_float[0]
    )
    key_lifted, key_pull = jax.vjp(
        feature_map, key_rows.astype(jnp.float32), weight_float[1], bias_float[1]
    )
    query_blocks = query_lifted.astype(jnp.bfloat16).reshape(blocks, BLOCK, heads_here, 2 * HD)
    key_blocks = key_lifted.astype(jnp.bfloat16).reshape(blocks, BLOCK, heads_here, 2 * HD)
    value_blocks = value_rows.reshape(blocks, BLOCK, heads_here, HD)
    block_state = jnp.einsum(
        "jthe,jthf->jhef", value_blocks, key_blocks, preferred_element_type=jnp.float32
    )
    block_norm = jnp.sum(key_blocks.astype(jnp.float32), axis=1)
    totals = (
        jnp.einsum("js,jhef->shef", member, block_state, precision=HIGHEST),
        jnp.einsum("js,jhf->shf", member, block_norm, precision=HIGHEST),
    )
    incoming = entering(
        (totals[0], totals[1]),
        "ctx",
        add_pair,
        (jnp.zeros_like(totals[0]), jnp.zeros_like(totals[1])),
        False,
    )
    state_before = jnp.einsum(
        "ji,ihef->jhef", earlier, block_state, precision=HIGHEST
    ) + jnp.einsum("js,shef->jhef", member, incoming[0], precision=HIGHEST)
    norm_before = jnp.einsum("ji,ihf->jhf", earlier, block_norm, precision=HIGHEST) + jnp.einsum(
        "js,shf->jhf", member, incoming[1], precision=HIGHEST
    )
    numerator = jnp.einsum(
        "jthf,jhef->jthe",
        query_blocks,
        state_before,
        precision=HIGHEST,
        preferred_element_type=jnp.float32,
    )
    denominator = jnp.einsum(
        "jthf,jhf->jth",
        query_blocks,
        norm_before,
        precision=HIGHEST,
        preferred_element_type=jnp.float32,
    )
    scores = jnp.einsum(
        "jthf,jshf->jhts", query_blocks, key_blocks, preferred_element_type=jnp.float32
    )
    scores_low = jnp.where(causal, scores, 0.0).astype(jnp.bfloat16)
    numerator = numerator + jnp.einsum(
        "jhts,jshe->jthe", scores_low, value_blocks, preferred_element_type=jnp.float32
    )
    denominator = denominator + jnp.swapaxes(jnp.sum(scores_low.astype(jnp.float32), axis=-1), 1, 2)
    attended = numerator / denominator[..., None]
    attended_low = attended.astype(jnp.bfloat16).reshape(piece_rows, heads_here * HD)
    attention_sum = lax.psum_scatter(
        jnp.dot(attended_low, output_weight, preferred_element_type=jnp.float32),
        "tp",
        scatter_dimension=0,
        tiled=True,
    )
    middle = inputs + attention_sum + output_bias.astype(jnp.float32)
    second_normed, second_pull = jax.vjp(
        layer_norm, middle, second_gain.astype(jnp.float32), second_bias.astype(jnp.float32)
    )
    second_low = second_normed.astype(jnp.bfloat16)
    second_rows = lax.all_gather(second_low, "tp", axis=0, tiled=True)
    hidden_input = jnp.dot(
        second_rows, inner_weight, preferred_element_type=jnp.float32
    ) + inner_bias.astype(jnp.float32)
    activated_float, curve_pull = jax.vjp(gaussian_unit, hidden_input)
    activated = activated_float.astype(jnp.bfloat16)
    branch_out = lax.psum_scatter(
        jnp.dot(activated, outer_weight, preferred_element_type=jnp.float32).astype(jnp.bfloat16),
        "tp",
        scatter_dimension=0,
        tiled=True,
    ).astype(jnp.float32)
    result = (middle + branch_out + outer_bias.astype(jnp.float32)).astype(jnp.bfloat16)
    upstream = cotangent.astype(jnp.float32)
    upstream_rows = lax.all_gather(cotangent, "tp", axis=0, tiled=True)
    outer_delta = jnp.einsum(
        "tf,td->fd", activated, upstream_rows, preferred_element_type=jnp.float32
    )
    activated_delta = jnp.einsum(
        "td,fd->tf", upstream_rows, outer_weight, preferred_element_type=jnp.float32
    )
    (hidden_delta,) = curve_pull(activated_delta)
    hidden_low = hidden_delta.astype(jnp.bfloat16)
    inner_bias_delta = jnp.sum(hidden_low.astype(jnp.float32), axis=0)
    inner_delta = jnp.einsum(
        "td,tf->df", second_rows, hidden_low, preferred_element_type=jnp.float32
    )
    second_delta = lax.psum_scatter(
        jnp.einsum("tf,df->td", hidden_low, inner_weight, preferred_element_type=jnp.float32),
        "tp",
        scatter_dimension=0,
        tiled=True,
    )
    middle_back, second_gain_part, second_bias_part = second_pull(second_delta)
    middle_delta = upstream + middle_back
    middle_low = middle_delta.astype(jnp.bfloat16)
    middle_rows = lax.all_gather(middle_low, "tp", axis=0, tiled=True)
    output_delta = jnp.einsum(
        "tk,td->kd", attended_low, middle_rows, preferred_element_type=jnp.float32
    )
    attended_delta = rounded(
        jnp.einsum("td,kd->tk", middle_rows, output_weight, preferred_element_type=jnp.float32)
    )
    attended_delta = attended_delta.reshape(blocks, BLOCK, heads_here, HD)
    numerator_delta = attended_delta / denominator[..., None]
    denominator_delta = -jnp.sum(attended_delta * attended, axis=-1) / denominator
    score_delta = (
        jnp.einsum(
            "jthe,jshe->jhts",
            numerator_delta,
            value_blocks,
            precision=HIGHEST,
            preferred_element_type=jnp.float32,
        )
        + jnp.swapaxes(denominator_delta, 1, 2)[..., None]
    )
    score_low = jnp.where(causal, score_delta, 0.0).astype(jnp.bfloat16)
    value_delta = jnp.einsum(
        "jhts,jthe->jshe",
        scores_low,
        numerator_delta,
        precision=HIGHEST,
        preferred_element_type=jnp.float32,
    )
    query_delta = (
        jnp.einsum("jhts,jshf->jthf", score_low, key_blocks, preferred_element_type=jnp.float32)
        + jnp.einsum(
            "jthe,jhef->jthf",
            numerator_delta,
            state_before,
            precision=HIGHEST,
            preferred_element_type=jnp.float32,
        )
        + denominator_delta[..., None] * norm_before[:, None]
    )
    key_delta = jnp.einsum(
        "jhts,jthf->jshf", score_low, query_blocks, preferred_element_type=jnp.float32
    )
    before_delta = jnp.einsum(
        "jthf,jthe->jhef",
        query_blocks,
        numerator_delta,
        precision=HIGHEST,
        preferred_element_type=jnp.float32,
    )
    norm_before_delta = jnp.einsum(
        "jthf,jth->jhf",
        query_blocks,
        denominator_delta,
        precision=HIGHEST,
        preferred_element_type=jnp.float32,
    )
    leaving = (
        jnp.einsum("js,jhef->shef", member, before_delta, precision=HIGHEST),
        jnp.einsum("js,jhf->shf", member, norm_before_delta, precision=HIGHEST),
    )
    later_sums = entering(
        (leaving[0], leaving[1]),
        "ctx",
        add_pair,
        (jnp.zeros_like(leaving[0]), jnp.zeros_like(leaving[1])),
        True,
    )
    state_delta = jnp.einsum(
        "ji,jhef->ihef", earlier, before_delta, precision=HIGHEST
    ) + jnp.einsum("js,shef->jhef", member, later_sums[0], precision=HIGHEST)
    block_norm_delta = jnp.einsum(
        "ji,jhf->ihf", earlier, norm_before_delta, precision=HIGHEST
    ) + jnp.einsum("js,shf->jhf", member, later_sums[1], precision=HIGHEST)
    value_delta = value_delta + jnp.einsum(
        "jhef,jthf->jthe",
        state_delta,
        key_blocks,
        precision=HIGHEST,
        preferred_element_type=jnp.float32,
    )
    key_delta = (
        key_delta
        + jnp.einsum(
            "jhef,jthe->jthf",
            state_delta,
            value_blocks,
            precision=HIGHEST,
            preferred_element_type=jnp.float32,
        )
        + block_norm_delta[:, None]
    )
    query_in_delta, query_weight_delta, query_bias_delta = query_pull(
        rounded(query_delta).reshape(piece_rows, heads_here, 2 * HD)
    )
    key_in_delta, key_weight_delta, key_bias_delta = key_pull(
        rounded(key_delta).reshape(piece_rows, heads_here, 2 * HD)
    )
    mixed_delta = jnp.stack(
        [query_in_delta, key_in_delta, value_delta.reshape(piece_rows, heads_here, HD)], axis=1
    )
    mixed_delta = mixed_delta.astype(jnp.bfloat16).reshape(piece_rows, 3 * heads_here * HD)
    mixer_bias_delta = jnp.sum(mixed_delta.astype(jnp.float32), axis=0).reshape(3, heads_here * HD)
    mixer_delta = jnp.einsum(
        "td,tk->dk", first_rows, mixed_delta, preferred_element_type=jnp.float32
    ).reshape(model_width, 3, heads_here * HD)
    first_delta = lax.psum_scatter(
        jnp.einsum("tk,dk->td", mixed_delta, mixer_flat, preferred_element_type=jnp.float32).astype(
            jnp.bfloat16
        ),
        "tp",
        scatter_dimension=0,
        tiled=True,
    ).astype(jnp.float32)
    input_back, first_gain_part, first_bias_part = first_pull(first_delta)
    tokens_delta = middle_delta + input_back
    feature_weight_delta = jnp.stack([query_weight_delta, key_weight_delta])
    feature_bias_delta = jnp.stack([query_bias_delta, key_bias_delta])
    output_bias_part = jnp.sum(middle_delta, axis=0)
    outer_bias_part = jnp.sum(upstream, axis=0)
    summed = lax.psum(
        (
            mixer_delta,
            mixer_bias_delta,
            feature_weight_delta,
            feature_bias_delta,
            output_delta,
            inner_delta,
            inner_bias_delta,
            outer_delta,
            first_gain_part,
            first_bias_part,
            output_bias_part,
            second_gain_part,
            second_bias_part,
            outer_bias_part,
        ),
        ("dp", "ctx"),
    )
    shared = lax.psum((summed[8], summed[9], summed[10], summed[11], summed[12], summed[13]), "tp")
    return (
        result,
        tokens_delta,
        shared[0],
        shared[1],
        summed[0],
        summed[1],
        summed[2],
        summed[3],
        summed[4],
        shared[2],
        shared[3],
        shared[4],
        summed[5],
        summed[6],
        summed[7],
        shared[5],
    )


def solution(mesh):
    in_specs = (
        P(("dp", "ctx", "tp"), None),
        P(),
        P(),
        P(None, None, "tp"),
        P(None, "tp"),
        P(None, "tp", None, None),
        P(None, "tp", None),
        P("tp", None),
        P(),
        P(),
        P(),
        P(None, "tp"),
        P("tp"),
        P("tp", None),
        P(),
        P("dp", None),
        P(("dp", "ctx", "tp"), None),
    )
    out_specs = (
        P(("dp", "ctx", "tp"), None),
        P(("dp", "ctx", "tp"), None),
        P(),
        P(),
        P(None, None, "tp"),
        P(None, "tp"),
        P(None, "tp", None, None),
        P(None, "tp", None),
        P("tp", None),
        P(),
        P(),
        P(),
        P(None, "tp"),
        P("tp"),
        P("tp", None),
        P(),
    )
    return jax.shard_map(shards, mesh=mesh, in_specs=in_specs, out_specs=out_specs, check_vma=False)
```

profile of v0, /device:TPU:0, one launch (start us, length us, event | category | flops | bytes accessed | tf_op | source)
XLA Modules:
  0.0 1006.3 jit_solution(10132067115701984201)
XLA Ops:
  14.2 65.0 %all-gather.11.cloned.1.call-done = bf16[2048,768]{1,0:T(8,128)(2,1)} async-done(((bf16[512,768]{1,0:T(8,128)(2,1)}), bf16[2048,768]{1,0:T(8,128)(2,1)}) %all-gather.11.cloned.1.call-update) | async-done | bytes 3145744 | tf_op jit(solution)/shard_map/all_gather | solution.py:95
  121.6 5.6 all-gather.4
  147.0 7.0 all-gather
  154.0 6.5 while.34
  161.7 5.7 multiply_add_fusion.3
  189.6 108.3 %reduce-scatter.5.cloned.1.call-done = f32[512,768]{1,0:T(8,128)} async-done(((f32[2048,768]{1,0:T(8,128)}), f32[512,768]{1,0:T(8,128)}) %reduce-scatter.5.cloned.1.call-update) | async-done | bytes 1572880 | tf_op jit(solution)/shard_map/reduce_scatter | solution.py:160
  303.6 62.3 %all-gather.13.cloned.1.call-done = bf16[2048,768]{1,0:T(8,128)(2,1)} async-done(((bf16[512,768]{1,0:T(8,128)(2,1)}), bf16[2048,768]{1,0:T(8,128)(2,1)}) %all-gather.13.cloned.1.call-update) | async-done | bytes 3145744 | tf_op jit(solution)/shard_map/all_gather | solution.py:171
  365.9 7.5 fusion.128
  373.4 56.1 %all-gather.15.cloned.1.call-done = bf16[2048,768]{1,0:T(8,128)(2,1)} async-done(((bf16[512,768]{1,0:T(8,128)(2,1)}), bf16[2048,768]{1,0:T(8,128)(2,1)}) %all-gather.15.cloned.1.call-update) | async-done | bytes 3145744 | tf_op jit(solution)/shard_map/all_gather | solution.py:185
  429.5 12.2 %convert_reduce_fusion = (f32[768]{0:T(1024)}, bf16[2048,768]{1,0:T(8,128)(2,1)S(1)}, bf16[2048,768]{1,0:T(8,128)(2,1)}) fusion(f32[2048,768]{1,0:T(8,128)} %fusion.128, f32[768]{0:T(1024)} %convert_element_type.136, bf16[2048,768]{1,0:T(8,128)(2,1)} %all-gather.15.cloned.1.call-done, bf16[768,768]{1,0:T(8,128)(2,1)S(1)} %copy-done), kind=kOutput, calls=%fused_computation.18 | convolution fusion | flops 2461531392 | bytes 16914432 | tf_op jit(solution)/shard_map/td,fd->tf/dot_general | solution.py:189
  448.1 6.3 convolution_convert_fusion
  455.0 102.6 %reduce-scatter.9.cloned.1.call-done = f32[512,768]{1,0:T(8,128)} async-done(((f32[2048,768]{1,0:T(8,128)}), f32[512,768]{1,0:T(8,128)}) %reduce-scatter.9.cloned.1.call-update) | async-done | bytes 1572880 | tf_op jit(solution)/shard_map/reduce_scatter | solution.py:198
  560.2 60.3 %reduce-scatter.7.cloned.1.call-done = bf16[512,768]{1,0:T(8,128)(2,1)} async-done(((bf16[2048,768]{1,0:T(8,128)(2,1)}), bf16[512,768]{1,0:T(8,128)(2,1)}) %reduce-scatter.7.cloned.1.call-update) | async-done | bytes 786448 | tf_op jit(solution)/shard_map/reduce_scatter | solution.py:177
  629.5 60.4 %all-gather.17.cloned.1.call-done = bf16[2048,768]{1,0:T(8,128)(2,1)} async-done(((bf16[512,768]{1,0:T(8,128)(2,1)}), bf16[2048,768]{1,0:T(8,128)(2,1)}) %all-gather.17.cloned.1.call-update) | async-done | bytes 3145744 | tf_op jit(solution)/shard_map/all_gather | solution.py:207
  695.6 5.2 multiply_reduce_fusion
  701.0 10.8 %fusion.23 = f32[32,3,128,64]{2,3,1,0:T(8,128)} fusion(f32[32,3,64,128]{3,0,2,1:T(8,128)S(1)} %copy-done.27, f32[32,64,3,64]{1,0,3,2:T(8,128)S(1)} %copy-done.24, f32[32,64,3]{1,2,0:T(4,128)S(1)} %copy-done.56), kind=kOutput, calls=%fused_computation.50 | convolution fusion | flops 604372992 | bytes 7888896 | tf_op jit(solution)/shard_map/jthe,jhef->jthf/dot_general | solution.py:237
  717.6 5.2 all-gather.5
  725.7 6.5 all-gather.2
  733.0 5.7 multiply_add_fusion.2
  810.5 7.0 fusion.132
  830.0 39.3 %reduce-scatter.11.cloned.1.call-done = bf16[512,768]{1,0:T(8,128)(2,1)} async-done(((bf16[2048,768]{1,0:T(8,128)(2,1)}), bf16[512,768]{1,0:T(8,128)(2,1)}) %reduce-scatter.11.cloned.1.call-update) | async-done | bytes 786448 | tf_op jit(solution)/shard_map/reduce_scatter | solution.py:312
  875.3 26.5 %all-reduce = (f32[768]{0:T(1024)S(1)}, f32[768]{0:T(1024)S(1)}, f32[3,192]{1,0:T(4,128)}, f32[2,3,64]{2,1,0:T(4,128)S(1)}, f32[768]{0:T(1024)S(1)}, /*index=5*/...) all-reduce(f32[768]{0:T(1024)S(1)} %get-tuple-element.373, ...), channel_id=1, replica_groups=mesh['dp'=2,'ctx'=4,'tp'=4] {'dp','ctx'}, use_global_device_ids=true, to_apply=%region_32.33 | all-reduce | flops 6336 | bytes 50688 | tf_op jit(solution)/shard_map/psum | solution.py:326
  902.4 18.5 %all-reduce.2 = (f32[768]{0:T(1024)}, f32[768]{0:T(1024)}, f32[768]{0:T(1024)}, f32[768]{0:T(1024)}, f32[768]{0:T(1024)}, /*index=5*/f32[768]{0:T(1024)}) all-reduce(f32[768]{0:T(1024)S(1)} %get-tuple-element.404, f32[768]{0:T(1024)S(1)} %get-tuple-element.405, ...), channel_id=1, replica_groups=mesh['dp'=2,'ctx'=4,'tp'=4] {'tp'}, use_global_device_ids=true, to_apply=%region_33.34 | all-reduce | flops 4608 | bytes 36864 | tf_op jit(solution)/shard_map/psum | solution.py:345
  920.9 70.3 %all-reduce.5.cloned.1.call-done = (f32[768,3,192]{0,2,1:T(8,128)}, f32[2,3,64,64]{3,2,1,0:T(8,128)}, f32[192,768]{1,0:T(8,128)}, f32[768,768]{1,0:T(8,128)}, f32[768,768]{1,0:T(8,128)}) async-done(((f32[768,3,192]{0,2,1:T(8,128)}, f32[2,3,64,64]{3,2,1,0:T(8,128)}, f32[192,768]{1,0:T(8,128)}, f32[768,768]{1,0:T(8,128)}, f32[768,768]{1,0:T(8,128)}), (f32[768,3,192]{0,2,1:T(8,128)}, ...) | async-done | bytes 7176208 | tf_op jit(solution)/shard_map/psum | solution.py:326
  (377 shorter events, 236.6 us)
Async XLA Ops:
  7.2 422.3 %copy-start = (bf16[768,768]{1,0:T(8,128)(2,1)S(1)}, bf16[768,768]{1,0:T(8,128)(2,1)}, u32[]{:S(2)}) copy-start(bf16[768,768]{1,0:T(8,128)(2,1)} %param.34) | copy-start | bytes 3538948
  7.2 72.0 %all-gather.11.cloned.1.call-start = ((), (), s32[]{:S(2)}) async-start(), calls=%async_computation.4 | async-start | bytes 3932160 | tf_op jit(solution)/shard_map/all_gather | solution.py:95
  8.8 70.4 %copy-start.98 = (bf16[768,3,192]{0,2,1:T(8,128)(2,1)S(1)}, bf16[768,3,192]{0,2,1:T(8,128)(2,1)}, u32[]{:S(2)}) copy-start(bf16[768,3,192]{0,2,1:T(8,128)(2,1)} %param.24) | copy-start | bytes 2654212
  12.8 285.1 %reduce-scatter.5.cloned.1.call-start = ((), (), s32[]{:S(2)}) async-start(), calls=%async_computation.5 | async-start | bytes 7864320 | tf_op jit(solution)/shard_map/reduce_scatter | solution.py:160
  87.5 22.8 %copy-start.5 = (f32[2048,3,64]{0,2,1:T(8,128)}, f32[2048,3,64]{0,2,1:T(8,128)S(1)}, u32[]{:S(2)}) copy-start(f32[2048,3,64]{0,2,1:T(8,128)S(1)} %get-tuple-element.454) | copy-start | bytes 4718596
  117.1 10.1 %copy-start.11 = (f32[2048,3,64]{0,2,1:T(8,128)S(1)}, f32[2048,3,64]{0,2,1:T(8,128)}, u32[]{:S(2)}) copy-start(f32[2048,3,64]{0,2,1:T(8,128)} %get-tuple-element.448) | copy-start | bytes 4718596
  117.1 10.1 %copy-start.48 = (f32[2048,3]{0,1:T(4,128)S(1)}, f32[2048,3]{0,1:T(4,128)}, u32[]{:S(2)}) copy-start(f32[2048,3]{0,1:T(4,128)} %get-tuple-element.447) | copy-start | bytes 73732
  188.3 177.6 %all-gather.13.cloned.1.call-start = ((), (), s32[]{:S(2)}) async-start(), calls=%async_computation.6 | async-start | bytes 3932160 | tf_op jit(solution)/shard_map/all_gather | solution.py:171
  301.7 127.8 %all-gather.15.cloned.1.call-start = ((), (), s32[]{:S(2)}) async-start(), calls=%async_computation.8 | async-start | bytes 3932160 | tf_op jit(solution)/shard_map/all_gather | solution.py:185
  302.3 255.3 %reduce-scatter.9.cloned.1.call-start = ((), (), s32[]{:S(2)}) async-start(), calls=%async_computation.9 | async-start | bytes 7864320 | tf_op jit(solution)/shard_map/reduce_scatter | solution.py:198
  429.5 13.9 %copy-start.97 = (bf16[768,768]{1,0:T(8,128)(2,1)S(1)}, bf16[768,768]{1,0:T(8,128)(2,1)}, u32[]{:S(2)}) copy-start(bf16[768,768]{1,0:T(8,128)(2,1)} %param.32) | copy-start | bytes 3538948
  448.0 172.5 %reduce-scatter.7.cloned.1.call-start = ((), (), s32[]{:S(2)}) async-start(), calls=%async_computation.7 | async-start | bytes 3932160 | tf_op jit(solution)/shard_map/reduce_scatter | solution.py:177
  454.4 235.5 %all-gather.17.cloned.1.call-start = ((), (), s32[]{:S(2)}) async-start(), calls=%async_computation.10 | async-start | bytes 3932160 | tf_op jit(solution)/shard_map/all_gather | solution.py:207
  455.0 105.2 %copy-start.79 = (f32[512]{0:T(512)S(1)}, f32[512]{0:T(512)}, u32[]{:S(2)}) copy-start(f32[512]{0:T(512)} %copy-done.78) | copy-start | bytes 6148
  560.2 64.8 %copy-start.32 = (bf16[512,768]{1,0:T(8,128)(2,1)S(1)}, bf16[512,768]{1,0:T(8,128)(2,1)}, u32[]{:S(2)}) copy-start(bf16[512,768]{1,0:T(8,128)(2,1)} %param.37) | copy-start | bytes 2359300
  625.0 64.9 %copy-start.53 = (bf16[192,768]{1,0:T(8,128)(2,1)S(1)}, bf16[192,768]{1,0:T(8,128)(2,1)}, u32[]{:S(2)}) copy-start(bf16[192,768]{1,0:T(8,128)(2,1)} %param.28) | copy-start | bytes 884740
  626.2 243.1 %reduce-scatter.11.cloned.1.call-start = ((), (), s32[]{:S(2)}) async-start(), calls=%async_computation.11 | async-start | bytes 3932160 | tf_op jit(solution)/shard_map/reduce_scatter | solution.py:312
  701.0 10.8 %copy-start.23 = (bf16[32,64,3,128]{3,1,2,0:T(8,128)(2,1)S(1)}, bf16[32,64,3,128]{3,1,2,0:T(8,128)(2,1)}, u32[]{:S(2)}) copy-start(bf16[32,64,3,128]{3,1,2,0:T(8,128)(2,1)} %copy-done.22) | copy-start | bytes 4718596
  810.2 181.0 %all-reduce.5.cloned.1.call-start = ((), (), s32[]{:S(2)}) async-start(), calls=%async_computation.12 | async-start | bytes 14548992 | tf_op jit(solution)/shard_map/psum | solution.py:326
  829.8 39.5 %copy-start.68 = (f32[768]{0:T(1024)S(1)}, f32[768]{0:T(1024)}, u32[]{:S(2)}) copy-start(f32[768]{0:T(1024)} %copy-done.67) | copy-start | bytes 9220
  829.8 39.5 %copy-start.70 = (f32[512]{0:T(512)S(1)}, f32[512]{0:T(512)}, u32[]{:S(2)}) copy-start(f32[512]{0:T(512)} %copy-done.69) | copy-start | bytes 6148
  829.9 41.3 %copy-start.77 = (f32[512]{0:T(512)S(1)}, f32[512]{0:T(512)}, u32[]{:S(2)}) copy-start(f32[512]{0:T(512)} %copy-done.76) | copy-start | bytes 6148
  829.9 41.3 %copy-start.74 = (f32[512]{0:T(512)S(1)}, f32[512]{0:T(512)}, u32[]{:S(2)}) copy-start(f32[512]{0:T(512)} %copy-done.73) | copy-start | bytes 6148
  830.0 43.3 %copy-start.19 = (f32[512,768]{1,0:T(8,128)S(1)}, f32[512,768]{1,0:T(8,128)}, u32[]{:S(2)}) copy-start(f32[512,768]{1,0:T(8,128)} %copy-done.18) | copy-start | bytes 4718596
  (89 other events, 322.9 us)
Sparse Core Ops, SparseCore 0:
  12.9 66.1 all-gather.10
  188.4 109.4 reduce-scatter.4
  301.8 64.0 all-gather.12
  367.3 62.1 all-gather.14
  448.2 109.3 reduce-scatter.8
  559.8 60.7 reduce-scatter.6
  626.3 63.5 all-gather.16
  810.4 58.9 reduce-scatter.10
  874.4 116.7 all-reduce.4
where the time goes:
time: 1020 us; the launch traced here: 1010 us
  waiting for transfers between devices  625 us (61%)
  matrix products  136 us (13%)
  local copies, waits for them, and re-layouts  86.1 us (8%)
  other arithmetic  72.6 us (7%)
  blocking collectives  69.3 us (7%)
  between operations  15.4 us (2%)
    reduce_scatter x1, waiting for transfers between devices, shards(): lax.psum_scatter(jnp.dot(attended_low, output_weight, preferred_element_t...  108 us
    reduce_scatter x1, waiting for transfers between devices, shards(): lax.psum_scatter(jnp.einsum('tf,df->td', hidden_low, inner_weight, prefer...  103 us
    psum x1, waiting for transfers between devices, shards(): lax.psum((mixer_delta, mixer_bias_delta, feature_weight_delta, feature_bi...  70.3 us
    all_gather x1, waiting for transfers between devices, shards(): first_rows = lax.all_gather(first_low, 'tp', axis=0, tiled=True)  65 us
    all_gather x1, waiting for transfers between devices, shards(): second_rows = lax.all_gather(second_low, 'tp', axis=0, tiled=True)  62.3 us
    all_gather x1, waiting for transfers between devices, shards(): middle_rows = lax.all_gather(middle_low, 'tp', axis=0, tiled=True)  60.4 us
    reduce_scatter x1, waiting for transfers between devices, shards(): lax.psum_scatter(jnp.dot(activated, outer_weight, preferred_element_type=...  60.3 us
    all_gather x1, waiting for transfers between devices, shards(): upstream_rows = lax.all_gather(cotangent, 'tp', axis=0, tiled=True)  56.1 us
  transfers between devices with their start and end apart: 9, of which 9 were waited for; matrix products, arithmetic and copies ran while one was open for 5% of the time, Pallas kernels for 0%

commit v1 on v0

--- a/solution.py
+++ b/solution.py
@@ -2,6 +2,7 @@
 import jax.numpy as jnp
 from jax import lax
 from jax.sharding import PartitionSpec as P
+from jax.lax import psum
 
 HD = 64
 BLOCK = 64
@@ -323,24 +324,27 @@
     feature_bias_delta = jnp.stack([query_bias_delta, key_bias_delta])
     output_bias_part = jnp.sum(middle_delta, axis=0)
     outer_bias_part = jnp.sum(upstream, axis=0)
-    summed = lax.psum(
-        (
-            mixer_delta,
-            mixer_bias_delta,
-            feature_weight_delta,
-            feature_bias_delta,
-            output_delta,
-            inner_delta,
-            inner_bias_delta,
-            outer_delta,
-            first_gain_part,
-            first_bias_part,
-            output_bias_part,
-            second_gain_part,
-            second_bias_part,
-            outer_bias_part,
+    summed = psum(
+        psum(
+            (
+                mixer_delta,
+                mixer_bias_delta,
+                feature_weight_delta,
+                feature_bias_delta,
+                output_delta,
+                inner_delta,
+                inner_bias_delta,
+                outer_delta,
+                first_gain_part,
+                first_bias_part,
+                output_bias_part,
+                second_gain_part,
+                second_bias_part,
+                outer_bias_part,
+            ),
+            "ctx",
         ),
-        ("dp", "ctx"),
+        "dp",
     )
     shared = lax.psum((summed[8], summed[9], summed[10], summed[11], summed[12], summed[13]), "tp")
     return (

time: 1020 us -> 1220 us (1.20)
  waiting for transfers between devices: 625 us -> 828 us
    psum x1 -> x2, waiting for transfers between devices: 70.3 us -> 261 us  [the longest x1 133 us: shards(): psum(psum((mixer_delta, mixer_bias_delta, feature_weight_delta, feature_b...]
    reduce_scatter x1, waiting for transfers between devices: 39.3 us -> 62.8 us  [shards(): lax.psum_scatter(jnp.einsum('tk,dk->td', mixed_delta, mixer_flat, preferr...]
    psum x1 -> x2, blocking collectives: 26.5 us -> 21.9 us  [the longest x1 11.9 us: shards(): psum((mixer_delta, mixer_bias_delta, feature_weight_delta, feature_bias_d...]
    unnamed x220 -> x214, local copies, waits for them, and re-layouts: 31.8 us -> 32.7 us
  transfers between devices with their start and end apart: 9 -> 10, of which waited for: 9 -> 10; matrix products, arithmetic and copies ran while one was open for 5% -> 4% of each run, Pallas kernels for 0% -> 0%
where the time goes in v1:
time: 1220 us; the launch traced here: 1210 us
  waiting for transfers between devices  828 us (68%)
  matrix products  141 us (12%)
  local copies, waits for them, and re-layouts  86.3 us (7%)
  other arithmetic  74.4 us (6%)
  blocking collectives  64.6 us (5%)
  between operations  15.6 us (1%)
    psum x1, waiting for transfers between devices, shards(): psum(psum((mixer_delta, mixer_bias_delta, feature_weight_delta, feature_b...  133 us
    psum x1, waiting for transfers between devices, shards(): psum((mixer_delta, mixer_bias_delta, feature_weight_delta, feature_bias_d...  128 us
    reduce_scatter x1, waiting for transfers between devices, shards(): lax.psum_scatter(jnp.dot(attended_low, output_weight, preferred_element_t...  108 us
    reduce_scatter x1, waiting for transfers between devices, shards(): lax.psum_scatter(jnp.einsum('tf,df->td', hidden_low, inner_weight, prefer...  102 us
    all_gather x1, waiting for transfers between devices, shards(): first_rows = lax.all_gather(first_low, 'tp', axis=0, tiled=True)  65 us
    reduce_scatter x1, waiting for transfers between devices, shards(): lax.psum_scatter(jnp.einsum('tk,dk->td', mixed_delta, mixer_flat, preferr...  62.8 us
    all_gather x1, waiting for transfers between devices, shards(): second_rows = lax.all_gather(second_low, 'tp', axis=0, tiled=True)  62.3 us
    reduce_scatter x1, waiting for transfers between devices, shards(): lax.psum_scatter(jnp.dot(activated, outer_weight, preferred_element_type=...  60.3 us
  transfers between devices with their start and end apart: 10, of which 10 were waited for; matrix products, arithmetic and copies ran while one was open for 4% of the time, Pallas kernels for 0%

profile of v1, /device:TPU:0, one launch (start us, length us, event | category | flops | bytes accessed | tf_op | source)
XLA Modules:
  0.0 1210.2 jit_solution(12297158764987863730)
XLA Ops:
  14.2 65.0 %all-gather.11.cloned.1.call-done = bf16[2048,768]{1,0:T(8,128)(2,1)} async-done(((bf16[512,768]{1,0:T(8,128)(2,1)}), bf16[2048,768]{1,0:T(8,128)(2,1)}) %all-gather.11.cloned.1.call-update) | async-done | bytes 3145744 | tf_op jit(solution)/shard_map/all_gather | solution.py:96
  146.7 7.0 all-gather
  153.7 6.6 while.34
  161.4 5.7 multiply_add_fusion.3
  189.3 108.3 %reduce-scatter.5.cloned.1.call-done = f32[512,768]{1,0:T(8,128)} async-done(((f32[2048,768]{1,0:T(8,128)}), f32[512,768]{1,0:T(8,128)}) %reduce-scatter.5.cloned.1.call-update) | async-done | bytes 1572880 | tf_op jit(solution)/shard_map/reduce_scatter | solution.py:161
  303.3 62.3 %all-gather.13.cloned.1.call-done = bf16[2048,768]{1,0:T(8,128)(2,1)} async-done(((bf16[512,768]{1,0:T(8,128)(2,1)}), bf16[2048,768]{1,0:T(8,128)(2,1)}) %all-gather.13.cloned.1.call-update) | async-done | bytes 3145744 | tf_op jit(solution)/shard_map/all_gather | solution.py:172
  365.6 7.5 fusion.128
  373.1 56.1 %all-gather.15.cloned.1.call-done = bf16[2048,768]{1,0:T(8,128)(2,1)} async-done(((bf16[512,768]{1,0:T(8,128)(2,1)}), bf16[2048,768]{1,0:T(8,128)(2,1)}) %all-gather.15.cloned.1.call-update) | async-done | bytes 3145744 | tf_op jit(solution)/shard_map/all_gather | solution.py:186
  429.2 12.3 %convert_reduce_fusion = (f32[768]{0:T(1024)}, bf16[2048,768]{1,0:T(8,128)(2,1)S(1)}, bf16[2048,768]{1,0:T(8,128)(2,1)}) fusion(f32[2048,768]{1,0:T(8,128)} %fusion.128, f32[768]{0:T(1024)} %convert_element_type.136, bf16[2048,768]{1,0:T(8,128)(2,1)} %all-gather.15.cloned.1.call-done, bf16[768,768]{1,0:T(8,128)(2,1)S(1)} %copy-done), kind=kOutput, calls=%fused_computation.18 | convolution fusion | flops 2461531392 | bytes 16914432 | tf_op jit(solution)/shard_map/td,fd->tf/dot_general | solution.py:190
  447.9 6.2 convolution_convert_fusion
  454.8 102.5 %reduce-scatter.9.cloned.1.call-done = f32[512,768]{1,0:T(8,128)} async-done(((f32[2048,768]{1,0:T(8,128)}), f32[512,768]{1,0:T(8,128)}) %reduce-scatter.9.cloned.1.call-update) | async-done | bytes 1572880 | tf_op jit(solution)/shard_map/reduce_scatter | solution.py:199
  559.9 60.3 %reduce-scatter.7.cloned.1.call-done = bf16[512,768]{1,0:T(8,128)(2,1)} async-done(((bf16[2048,768]{1,0:T(8,128)(2,1)}), bf16[512,768]{1,0:T(8,128)(2,1)}) %reduce-scatter.7.cloned.1.call-update) | async-done | bytes 786448 | tf_op jit(solution)/shard_map/reduce_scatter | solution.py:178
  629.0 7.1 fusion.132
  640.3 49.2 %all-gather.17.cloned.1.call-done = bf16[2048,768]{1,0:T(8,128)(2,1)} async-done(((bf16[512,768]{1,0:T(8,128)(2,1)}), bf16[2048,768]{1,0:T(8,128)(2,1)}) %all-gather.17.cloned.1.call-update) | async-done | bytes 3145744 | tf_op jit(solution)/shard_map/all_gather | solution.py:208
  700.6 10.7 fusion.23
  725.4 6.5 all-gather.2
  738.1 6.5 fusion.15
  818.1 6.0 convolution_convert_fusion.1
  824.2 127.9 %all-reduce.8.cloned.1.call-done = (f32[768,3,192]{0,2,1:T(8,128)}, f32[2,3,64,64]{3,2,1,0:T(8,128)}, f32[192,768]{1,0:T(8,128)}, f32[768,768]{1,0:T(8,128)}, f32[768,768]{1,0:T(8,128)}) async-done(((f32[768,3,192]{0,2,1:T(8,128)}, f32[2,3,64,64]{3,2,1,0:T(8,128)}, f32[192,768]{1,0:T(8,128)}, f32[768,768]{1,0:T(8,128)}, f32[768,768]{1,0:T(8,128)}), (f32[768,3,192]{0,2,1:T(8,128)}, ...) | async-done | bytes 7176208 | tf_op jit(solution)/shard_map/psum | solution.py:328
  952.2 62.8 %reduce-scatter.11.cloned.1.call-done = bf16[512,768]{1,0:T(8,128)(2,1)} async-done(((bf16[2048,768]{1,0:T(8,128)(2,1)}), bf16[512,768]{1,0:T(8,128)(2,1)}) %reduce-scatter.11.cloned.1.call-update) | async-done | bytes 786448 | tf_op jit(solution)/shard_map/reduce_scatter | solution.py:313
  1021.1 11.9 all-reduce.1
  1033.0 10.0 all-reduce.3
  1043.6 18.6 %all-reduce = (f32[768]{0:T(1024)}, f32[768]{0:T(1024)}, f32[768]{0:T(1024)}, f32[768]{0:T(1024)}, f32[768]{0:T(1024)}, /*index=5*/f32[768]{0:T(1024)}) all-reduce(f32[768]{0:T(1024)S(1)} %get-tuple-element.424, f32[768]{0:T(1024)S(1)} %get-tuple-element.425, ...), channel_id=1, replica_groups=mesh['dp'=2,'ctx'=4,'tp'=4] {'tp'}, use_global_device_ids=true, to_apply=%region_34.35 | all-reduce | flops 4608 | bytes 36864 | tf_op jit(solution)/shard_map/psum | solution.py:349
  1062.2 132.6 %all-reduce.10.cloned.1.call-done = (f32[768,3,192]{0,2,1:T(8,128)}, f32[2,3,64,64]{3,2,1,0:T(8,128)}, f32[192,768]{1,0:T(8,128)}, f32[768,768]{1,0:T(8,128)}, f32[768,768]{1,0:T(8,128)}) async-done(((f32[768,3,192]{0,2,1:T(8,128)}, f32[2,3,64,64]{3,2,1,0:T(8,128)}, f32[192,768]{1,0:T(8,128)}, f32[768,768]{1,0:T(8,128)}, f32[768,768]{1,0:T(8,128)}), (f32[768,3,192]{0,2,1:T(8,128)}, ...) | async-done | bytes 7176208 | tf_op jit(solution)/shard_map/psum | solution.py:327
  (375 shorter events, 251.5 us)
Async XLA Ops:
  7.2 422.0 %copy-start = (bf16[768,768]{1,0:T(8,128)(2,1)S(1)}, bf16[768,768]{1,0:T(8,128)(2,1)}, u32[]{:S(2)}) copy-start(bf16[768,768]{1,0:T(8,128)(2,1)} %param.34) | copy-start | bytes 3538948
  7.2 72.0 %all-gather.11.cloned.1.call-start = ((), (), s32[]{:S(2)}) async-start(), calls=%async_computation.4 | async-start | bytes 3932160 | tf_op jit(solution)/shard_map/all_gather | solution.py:96
  8.8 70.4 %copy-start.95 = (bf16[768,3,192]{0,2,1:T(8,128)(2,1)S(1)}, bf16[768,3,192]{0,2,1:T(8,128)(2,1)}, u32[]{:S(2)}) copy-start(bf16[768,3,192]{0,2,1:T(8,128)(2,1)} %param.24) | copy-start | bytes 2654212
  12.8 284.8 %reduce-scatter.5.cloned.1.call-start = ((), (), s32[]{:S(2)}) async-start(), calls=%async_computation.5 | async-start | bytes 7864320 | tf_op jit(solution)/shard_map/reduce_scatter | solution.py:161
  87.4 22.8 %copy-start.5 = (f32[2048,3,64]{0,2,1:T(8,128)}, f32[2048,3,64]{0,2,1:T(8,128)S(1)}, u32[]{:S(2)}) copy-start(f32[2048,3,64]{0,2,1:T(8,128)S(1)} %get-tuple-element.468) | copy-start | bytes 4718596
  117.1 9.8 copy-start.45
  188.0 177.6 %all-gather.13.cloned.1.call-start = ((), (), s32[]{:S(2)}) async-start(), calls=%async_computation.6 | async-start | bytes 3932160 | tf_op jit(solution)/shard_map/all_gather | solution.py:172
  301.4 127.8 %all-gather.15.cloned.1.call-start = ((), (), s32[]{:S(2)}) async-start(), calls=%async_computation.8 | async-start | bytes 3932160 | tf_op jit(solution)/shard_map/all_gather | solution.py:186
  302.0 255.3 %reduce-scatter.9.cloned.1.call-start = ((), (), s32[]{:S(2)}) async-start(), calls=%async_computation.9 | async-start | bytes 7864320 | tf_op jit(solution)/shard_map/reduce_scatter | solution.py:199
  429.2 13.9 %copy-start.94 = (bf16[768,768]{1,0:T(8,128)(2,1)S(1)}, bf16[768,768]{1,0:T(8,128)(2,1)}, u32[]{:S(2)}) copy-start(bf16[768,768]{1,0:T(8,128)(2,1)} %param.32) | copy-start | bytes 3538948
  447.7 172.5 %reduce-scatter.7.cloned.1.call-start = ((), (), s32[]{:S(2)}) async-start(), calls=%async_computation.7 | async-start | bytes 3932160 | tf_op jit(solution)/shard_map/reduce_scatter | solution.py:178
  454.1 235.3 %all-gather.17.cloned.1.call-start = ((), (), s32[]{:S(2)}) async-start(), calls=%async_computation.10 | async-start | bytes 3932160 | tf_op jit(solution)/shard_map/all_gather | solution.py:208
  454.8 105.1 %copy-start.76 = (f32[512]{0:T(512)S(1)}, f32[512]{0:T(512)}, u32[]{:S(2)}) copy-start(f32[512]{0:T(512)} %copy-done.75) | copy-start | bytes 6148
  559.9 64.7 %copy-start.29 = (bf16[512,768]{1,0:T(8,128)(2,1)S(1)}, bf16[512,768]{1,0:T(8,128)(2,1)}, u32[]{:S(2)}) copy-start(bf16[512,768]{1,0:T(8,128)(2,1)} %param.37) | copy-start | bytes 2359300
  625.8 326.3 %all-reduce.8.cloned.1.call-start = ((), (), s32[]{:S(2)}) async-start(), calls=%async_computation.12 | async-start | bytes 14548992 | tf_op jit(solution)/shard_map/psum | solution.py:328
  636.1 53.3 %copy-start.50 = (bf16[192,768]{1,0:T(8,128)(2,1)S(1)}, bf16[192,768]{1,0:T(8,128)(2,1)}, u32[]{:S(2)}) copy-start(bf16[192,768]{1,0:T(8,128)(2,1)} %param.28) | copy-start | bytes 884740
  700.6 10.8 copy-start.19
  817.0 198.1 %reduce-scatter.11.cloned.1.call-start = ((), (), s32[]{:S(2)}) async-start(), calls=%async_computation.11 | async-start | bytes 3932160 | tf_op jit(solution)/shard_map/reduce_scatter | solution.py:313
  824.1 370.7 %all-reduce.10.cloned.1.call-start = ((), (), s32[]{:S(2)}) async-start(), calls=%async_computation.13 | async-start | bytes 14548992 | tf_op jit(solution)/shard_map/psum | solution.py:327
  952.1 63.0 %copy-start.65 = (f32[768]{0:T(1024)S(1)}, f32[768]{0:T(1024)}, u32[]{:S(2)}) copy-start(f32[768]{0:T(1024)} %copy-done.64) | copy-start | bytes 9220
  952.1 63.0 %copy-start.67 = (f32[512]{0:T(512)S(1)}, f32[512]{0:T(512)}, u32[]{:S(2)}) copy-start(f32[512]{0:T(512)} %copy-done.66) | copy-start | bytes 6148
  952.1 64.8 %copy-start.74 = (f32[512]{0:T(512)S(1)}, f32[512]{0:T(512)}, u32[]{:S(2)}) copy-start(f32[512]{0:T(512)} %copy-done.73) | copy-start | bytes 6148
  952.1 64.8 %copy-start.71 = (f32[512]{0:T(512)S(1)}, f32[512]{0:T(512)}, u32[]{:S(2)}) copy-start(f32[512]{0:T(512)} %copy-done.70) | copy-start | bytes 6148
  952.2 66.8 %copy-start.15 = (f32[512,768]{1,0:T(8,128)S(1)}, f32[512,768]{1,0:T(8,128)}, u32[]{:S(2)}) copy-start(f32[512,768]{1,0:T(8,128)} %copy-done.14) | copy-start | bytes 4718596
  (87 other events, 325.2 us)
Sparse Core Ops, SparseCore 0:
  12.9 66.1 all-gather.10
  188.1 109.4 reduce-scatter.4
  301.5 64.0 all-gather.12
  367.0 62.1 all-gather.14
  447.8 109.3 reduce-scatter.8
  559.4 60.7 reduce-scatter.6
  625.9 63.5 all-gather.16
  817.1 134.9 all-reduce.7
  954.5 60.5 reduce-scatter.10
  1018.1 176.7 all-reduce.9
